TPU v7x, 256 devices: a whole 4x4x8 slice. The times are simulated.
256 devices in a mesh: group: 8 (over x, z_lo), replica: 32 (over y, z_hi, core).
Axes of the slice: x: 4, y: 4, z: 8 (z_hi: 4, z_lo: 2; z = z_hi * 2 + z_lo), core: 2. Of those that a mesh axis runs over, the one named last changes fastest.
Arguments:
- hidden_in: bfloat16 [81920, 3072], P(('group', 'replica')), may hold values from -24 to 24
- w_query: bfloat16 [3072, 1536], replicated, may hold values from -0.109375 to 0.109375
- query_gain: float32 [128], replicated, may hold values from 0.5 to 2
- down_projection_matrix: bfloat16 [3072, 64], replicated, may hold values from -0.23925781 to 0.23925781
- up_projection_matrix: bfloat16 [64, 1536], replicated, may hold values from -0.59765625 to 0.59765625
- query_cotangent: bfloat16 [81920, 1536], P(('group', 'replica')), may hold values from -24 to 24
- first_moment: float32 [4608, 64], P(('group', 'replica')), may hold values from -3 to 3
- second_moment: float32 [4608, 64], P(('group', 'replica')), may hold values from 0.001 to 0.1
Outputs:
- new_down: bfloat16 [3072, 64], replicated
- new_up: bfloat16 [64, 1536], replicated
- first_next: float32 [4608, 64], P(('group', 'replica'))
- second_next: float32 [4608, 64], P(('group', 'replica'))
All inputs are finite; a program needn't handle non-finite values.
Results may differ from a plain program's by a relative error of at most 0.0019.
Values may be sent and summed in bfloat16 or wider, within the bound.
A program may use at most 64 MiB of HBM per device.

v0:
```python
import jax
import jax.numpy as jnp
from jax import lax
from jax.sharding import PartitionSpec as P

adapter_scale_factor = 0.5
norm_epsilon = 1e-06
beta_one = 0.9
beta_two = 0.999
first_bias = 1.0 - 0.9**10
second_bias = 1.0 - 0.999**10
learn_rate = 0.001
adam_eps = 1e-08


def queries_backward(
    rows_in, grads_in, w_query, query_gain, down_projection_matrix, up_projection_matrix
):
    reduced_rank_input = jnp.dot(
        rows_in, down_projection_matrix, preferred_element_type=jnp.float32
    ).astype(jnp.bfloat16)
    apply_projection = jnp.dot(rows_in, w_query, preferred_element_type=jnp.float32)
    apply_projection = apply_projection + adapter_scale_factor * jnp.dot(
        reduced_rank_input, up_projection_matrix, preferred_element_type=jnp.float32
    )
    token_count = apply_projection.shape[0]
    head_size = query_gain.shape[0]
    shaped = apply_projection.reshape(token_count, -1, head_size)
    inverse = lax.rsqrt(jnp.mean(shaped * shaped, axis=-1, keepdims=True) + norm_epsilon)
    normed = shaped * inverse
    upstream = grads_in.astype(jnp.float32).reshape(shaped.shape) * query_gain
    grad_pre = inverse * (upstream - normed * jnp.mean(upstream * normed, axis=-1, keepdims=True))
    grad_pre = grad_pre.reshape(token_count, -1).astype(jnp.bfloat16)
    backward_reduced = lax.dot_general(
        grad_pre, up_projection_matrix, (((1,), (1,)), ((), ())), preferred_element_type=jnp.float32
    )
    backward_reduced = (adapter_scale_factor * backward_reduced).astype(jnp.bfloat16)
    scaled_reduced = (reduced_rank_input.astype(jnp.float32) * adapter_scale_factor).astype(
        jnp.bfloat16
    )
    return (grad_pre, backward_reduced, scaled_reduced)


def adam_update(grads, params, first, second):
    first_new = beta_one * first + (1.0 - beta_one) * grads
    second_new = beta_two * second + (1.0 - beta_two) * grads * grads
    direction = first_new / first_bias / (jnp.sqrt(second_new / second_bias) + adam_eps)
    return ((params - learn_rate * direction).astype(jnp.bfloat16), first_new, second_new)


def on_device(
    hidden_in,
    w_query,
    query_gain,
    down_projection_matrix,
    up_projection_matrix,
    query_cotangent,
    first_moment,
    second_moment,
):
    model_width = hidden_in.shape[1]
    adapter_rank_size = down_projection_matrix.shape[1]
    row_count_total = model_width + up_projection_matrix.shape[1]
    accelerator_list = lax.axis_size("group") * lax.axis_size("replica")
    own_rows = row_count_total // accelerator_list
    grad_pre, backward_reduced, scaled_reduced = queries_backward(
        hidden_in,
        query_cotangent,
        w_query,
        query_gain,
        down_projection_matrix,
        up_projection_matrix,
    )
    stacked = jnp.concatenate([hidden_in, grad_pre], axis=1)
    operand = jnp.concatenate([backward_reduced, scaled_reduced], axis=1)
    matrix_product = lax.dot_general(
        stacked, operand, (((0,), (0,)), ((), ())), preferred_element_type=jnp.float32
    )
    row_ids = lax.iota(jnp.int32, lax.axis_size(("group", "replica")) * own_rows)
    is_down_matrix = (row_ids < model_width)[:, None]
    grad_own = lax.psum_scatter(
        jnp.where(
            is_down_matrix,
            matrix_product[:, :adapter_rank_size],
            matrix_product[:, adapter_rank_size:],
        )
        / accelerator_list,
        ("group", "replica"),
        scatter_dimension=0,
        tiled=True,
    )
    owner = lax.axis_index(("group", "replica"))
    combined = jnp.concatenate([down_projection_matrix, up_projection_matrix.T], axis=0)
    params_own = lax.dynamic_slice_in_dim(combined, owner * own_rows, own_rows, 0).astype(
        jnp.float32
    )
    updated_own, first_new, second_new = adam_update(
        grad_own, params_own, first_moment, second_moment
    )
    gathered = lax.all_gather(updated_own, ("group", "replica"), axis=0, tiled=True)
    return (gathered[:model_width], gathered[model_width:].T, first_new, second_new)


def solution(mesh):
    placed = (
        P(("group", "replica"), None),
        P(),
        P(),
        P(),
        P(),
        P(("group", "replica"), None),
        P(("group", "replica"), None),
        P(("group", "replica"), None),
    )
    return jax.shard_map(
        on_device,
        mesh=mesh,
        in_specs=placed,
        out_specs=(P(), P(), P(("group", "replica"), None), P(("group", "replica"), None)),
        check_vma=False,
    )
```

profile of v0, /device:TPU:1, one launch (start us, length us, event | category | flops | bytes accessed | tf_op | source)
XLA Modules:
  0.0 660.7 jit_solution(2586570845125717426)
XLA Ops:
  7.2 0.0 all-reduce.3.cloned.1.call-start
  7.2 3.1 multiply_convert_fusion.1
  10.3 5.8 fusion.15
  16.1 1.7 fusion.4
  17.8 2.0 copy.42
  19.8 0.2 multiply_reduce_fusion.1
  20.0 0.6 add_rsqrt_fusion
  20.6 0.4 copy-done.3
  21.0 1.7 copy.44
  22.7 0.7 broadcast_bitcast_fusion
  23.4 2.2 multiply_reduce_fusion
  25.6 0.2 mul.117
  25.7 1.9 copy.45
  27.6 2.3 mul.106
  29.9 3.1 copy.46
  33.1 3.0 multiply_convert_fusion
  36.1 0.4 fusion.6
  36.5 0.8 fusion
  37.3 0.0 copy-start.5
  37.3 1.2 fusion.5
  38.5 0.0 all-reduce.3.cloned.1.call-update
  38.5 0.4 copy.41
  38.9 0.2 copy.40
  39.2 261.5 %all-reduce.3.cloned.1.call-done = f32[4608,64]{0,1:T(8,128)} async-done(((f32[4608,64]{0,1:T(8,128)}), f32[4608,64]{0,1:T(8,128)}) %all-reduce.3.cloned.1.call-update) | async-done | bytes 1179664
  300.7 0.9 constant_dynamic-slice_fusion
  301.6 0.1 copy.47
  301.7 0.6 fusion.12
  302.3 349.1 %all-gather = bf16[256,18,64]{2,1,0:T(8,128)(2,1)S(1)} all-gather(bf16[1,18,64]{2,1,0:T(8,128)(2,1)S(1)} %get-tuple-element.20), channel_id=1, replica_groups=mesh['group'=8,'replica'=32] {'group','replica'}, dimensions={0}, use_global_device_ids=true | all-gather | bytes 592128 | tf_op jit(solution)/shard_map/all_gather | solution.py:100
  651.4 0.6 reshape.39
  651.9 0.1 slice.18
  652.0 1.0 copy.50
  653.0 0.8 copy.51
  (19 shorter events, 0.1 us)
Async XLA Ops:
  7.2 3.1 copy-start.1
  7.2 293.5 %all-reduce.3.cloned.1.call-start = ((), (), s32[]{:S(2)}) async-start(), calls=%async_computation | async-start | bytes 2359296
  10.3 5.8 copy-start.4
  19.8 1.2 copy-start.3
  29.9 3.1 copy-start
  33.0 3.5 copy-start.2
  33.1 3.5 copy-start.6
  37.3 1.2 copy-start.5
  38.5 263.2 %copy-start.7 = (f32[18,64]{1,0:T(8,128)S(1)}, f32[18,64]{1,0:T(8,128)}, u32[]{:S(2)}) copy-start(f32[18,64]{1,0:T(8,128)} %param.14) | copy-start | bytes 13828
  38.5 263.2 %copy-start.8 = (f32[18,64]{1,0:T(8,128)S(1)}, f32[18,64]{1,0:T(8,128)}, u32[]{:S(2)}) copy-start(f32[18,64]{1,0:T(8,128)} %param.15) | copy-start | bytes 13828
Sparse Core Ops, SparseCore 0:
  38.6 261.9 all-reduce.2
where the time goes:
time: 661 us
  blocking collectives  349 us (53%)
  waiting for transfers between devices  262 us (40%)
  local copies, waits for them, and re-layouts  16.3 us (2%)
  between operations  14.2 us (2%)
  matrix products  11.7 us (2%)
  other arithmetic  7.86 us (1%)
    all_gather x1, blocking collectives, on_device(): lax.all_gather(updated_own, ('group', 'replica'), axis=0, tiled=True)  349 us
    unnamed x2, waiting for transfers between devices  262 us
  transfers between devices with their start and end apart: 1, of which 1 were waited for; matrix products, arithmetic and copies ran while one was open for 0% of the time, Pallas kernels for 0%

commit v1 on v0

--- a/solution.py
+++ b/solution.py
@@ -97,7 +97,15 @@
     updated_own, first_new, second_new = adam_update(
         grad_own, params_own, first_moment, second_moment
     )
-    gathered = lax.all_gather(updated_own, ("group", "replica"), axis=0, tiled=True)
+    gathered = jnp.concatenate(
+        lax.all_to_all(
+            jnp.stack([updated_own for _ in range(lax.axis_size(("group", "replica")))]),
+            ("group", "replica"),
+            0,
+            0,
+        ),
+        axis=0,
+    )
     return (gathered[:model_width], gathered[model_width:].T, first_new, second_new)
 
 

time: 661 us -> 349 us (0.53)
  blocking collectives: 349 us -> 34.9 us
    all_gather x1 -> x0, blocking collectives: 349 us -> none  [on_device(): lax.all_gather(updated_own, ('group', 'replica'), axis=0, tiled=True)]
    all_to_all x0 -> x1, blocking collectives: none -> 34.9 us  [on_device(): lax.all_to_all(jnp.stack([updated_own for _ in range(lax.axis_size(('grou...]
where the time goes in v1:
time: 349 us
  waiting for transfers between devices  262 us (75%)
  blocking collectives  34.9 us (10%)
  local copies, waits for them, and re-layouts  18.4 us (5%)
  between operations  14.3 us (4%)
  matrix products  11.7 us (3%)
  other arithmetic  7.86 us (2%)
    unnamed x2, waiting for transfers between devices  262 us
    all_to_all x1, blocking collectives, on_device(): lax.all_to_all(jnp.stack([updated_own for _ in range(lax.axis_size(('grou...  34.9 us
  transfers between devices with their start and end apart: 1, of which 1 were waited for; matrix products, arithmetic and copies ran while one was open for 0% of the time, Pallas kernels for 0%

profile of v1, /device:TPU:1, one launch (start us, length us, event | category | flops | bytes accessed | tf_op | source)
XLA Modules:
  0.0 348.7 jit_solution(13554343984495735929)
XLA Ops:
  7.2 3.1 multiply_convert_fusion.1
  10.3 5.8 %fusion.14 = f32[320,1536]{1,0:T(8,128)S(1)} fusion(bf16[320,3072]{1,0:T(8,128)(2,1)S(1)} %copy-done.1, bf16[3072,1536]{1,0:T(8,128)(2,1)} %param.9), kind=kOutput, calls=%fused_computation.32 | convolution fusion | flops 3019898880 | bytes 13369344 | tf_op jit(solution)/shard_map/dot_general | solution.py:22
  16.1 1.7 fusion.4
  17.8 2.0 copy.42
  19.8 0.2 multiply_reduce_fusion.1
  20.0 0.6 add_rsqrt_fusion
  20.6 0.4 copy-done.3
  21.0 1.7 copy.44
  22.7 0.7 broadcast_bitcast_fusion
  23.4 2.2 multiply_reduce_fusion
  25.6 0.2 mul.117
  25.7 1.9 copy.45
  27.6 2.3 mul.106
  29.9 3.1 copy.46
  33.1 3.0 multiply_convert_fusion
  36.1 0.4 fusion.6
  36.5 0.8 fusion
  37.3 1.2 fusion.5
  38.5 0.4 copy.41
  38.9 0.2 copy.40
  39.2 261.5 %all-reduce.3.cloned.1.call-done = f32[4608,64]{0,1:T(8,128)} async-done(((f32[4608,64]{0,1:T(8,128)}), f32[4608,64]{0,1:T(8,128)}) %all-reduce.3.cloned.1.call-update) | async-done | bytes 1179664
  300.7 0.9 constant_dynamic-slice_fusion
  301.6 0.1 copy.47
  301.7 0.6 subtract_convert_fusion
  302.3 0.2 stack.2
  302.5 0.9 reshape.46
  303.4 34.9 %all_to_all.5 = bf16[256,2,576]{2,1,0:T(2,128)(2,1)S(1)} all-to-all(bf16[256,2,576]{2,1,0:T(2,128)(2,1)S(1)} %reshape.46), channel_id=1, replica_groups=mesh['group'=8,'replica'=32] {'group','replica'}, dimensions={0} | all-to-all | bytes 1179648 | tf_op jit(solution)/shard_map/all_to_all | solution.py:101
  338.3 1.0 reshape.47
  339.3 0.6 reshape.43
  339.9 0.1 slice.18
  340.0 1.0 copy.50
  341.0 0.8 copy.51
  (22 shorter events, 0.1 us)
Async XLA Ops:
  7.2 3.1 copy-start.1
  7.2 293.5 %all-reduce.3.cloned.1.call-start = ((), (), s32[]{:S(2)}) async-start(), calls=%async_computation.1 | async-start | bytes 2359296
  10.3 5.8 %copy-start.4 = (bf16[64,1536]{1,0:T(8,128)(2,1)S(1)}, bf16[64,1536]{1,0:T(8,128)(2,1)}, u32[]{:S(2)}) copy-start(bf16[64,1536]{1,0:T(8,128)(2,1)} %param.12) | copy-start | bytes 589828
  19.8 1.2 copy-start.3
  29.9 3.1 copy-start
  33.0 3.5 copy-start.2
  33.1 3.5 copy-start.6
  37.3 1.2 copy-start.5
  38.5 263.2 %copy-start.7 = (f32[18,64]{1,0:T(8,128)S(1)}, f32[18,64]{1,0:T(8,128)}, u32[]{:S(2)}) copy-start(f32[18,64]{1,0:T(8,128)} %param.14) | copy-start | bytes 13828
  38.5 263.2 %copy-start.8 = (f32[18,64]{1,0:T(8,128)S(1)}, f32[18,64]{1,0:T(8,128)}, u32[]{:S(2)}) copy-start(f32[18,64]{1,0:T(8,128)} %param.15) | copy-start | bytes 13828
Sparse Core Ops, SparseCore 0:
  38.6 261.9 all-reduce.2
